TPU v7x, 32 devices: a whole 2x2x4 slice. The times are simulated.
32 devices in a mesh: tm: 8 (over y, x, core), space: 4 (over z).
Axes of the slice: x: 2, y: 2, z: 4, core: 2. Of those that a mesh axis runs over, the one named last changes fastest.
Arguments:
- queries: bfloat16 [16384, 1536], P(('tm', 'space')), may hold values from -6 to 6
- key_rows: bfloat16 [16384, 1536], P(('tm', 'space')), may hold values from -6 to 6
- value_rows: bfloat16 [16384, 1536], P(('tm', 'space')), may hold values from -6 to 6
- block_list: int32 [128, 8], P(('tm', 'space')), may hold values from 0 to 127, as said below
- block_count: int32 [128], P(('tm', 'space')), may hold values from 1 to 8
Outputs:
- attended: bfloat16 [16384, 1536], P(('tm', 'space'))
Inputs may be any that keep to these rules, and one draw needn't show every extreme that they name: `block_list`: the candidates of query tile t, which lies in frame f = t // 16 at block p = t % 16 of the frame and in slab s = p // 4, are: the blocks of frame f with in-frame index from s * 4 - 1 to (s + 1) * 4 that lie within the frame; and, for each b from 0 to 2 and each of the frames f - 2**b and f + 2**b that lie within the clip, its blocks with in-frame index s * 4 + j where j runs over 0 to 3 with j % 2 == b % 2. Every entry of row t, padded ones included, is such a candidate, the entries of a row are distinct, and the first entry is block t itself.
All inputs are finite; a program needn't handle non-finite values.
Results may differ from a plain program's by a relative error of at most 0.0044.
Values may be sent and summed in bfloat16 or wider, within the bound.
A program may use at most 128 MiB of HBM per device.

v0:
```python
import jax
import jax.numpy as jnp
from jax import lax
from jax.sharding import PartitionSpec as P

HEAD = 128
BLOCK = 128


def with_halo(cells, sides, width):
    for axis, dim in sides:
        count = lax.axis_size(axis)
        ends = count - 1
        head = lax.slice_in_dim(cells, 0, width, axis=dim)
        tail = lax.slice_in_dim(cells, cells.shape[dim] - width, cells.shape[dim], axis=dim)
        cells = jnp.concatenate(
            [
                lax.ppermute(tail, axis, [(i, (i + 1) % count) for i in range(ends)]),
                cells,
                lax.ppermute(head, axis, [((i + 1) % count, i) for i in range(ends)]),
            ],
            axis=dim,
        )
    return cells


def from_behind(shard, axis, by):
    devices = lax.axis_size(axis)
    pairs = [(i, i + by) for i in range(devices) if 0 <= i + by < devices]
    return lax.ppermute(shard, axis, pairs)


def shards(queries, key_rows, value_rows, block_list, block_count):
    row_count, model_width = queries.shape
    blocks = row_count // BLOCK
    head_count = model_width // HEAD
    list_width = block_list.shape[1]
    inv_root = 1.0 / HEAD**0.5
    tm_count = lax.axis_size("tm")
    bit_total = tm_count.bit_length() - 1
    space_count = lax.axis_size("space")
    frame_index = lax.axis_index("tm")
    slab_index = lax.axis_index("space")
    frame_blocks = blocks * space_count
    first_block = frame_index * frame_blocks + slab_index * blocks
    paired = jnp.stack([key_rows, value_rows])
    widened = with_halo(paired, (("space", 1),), BLOCK)
    offsets = jnp.arange(blocks + 2, dtype=jnp.int32) - 1
    near_ok = ((offsets >= 0) | (slab_index > 0)) & (
        (offsets < blocks) | (slab_index < space_count - 1)
    )
    near_ids = jnp.where(near_ok, first_block + offsets, -1)
    shaped = paired.reshape(2, blocks // 2, 2, BLOCK, model_width)
    picks_base = 2 * jnp.arange(blocks // 2, dtype=jnp.int32)
    groups = [(widened.reshape(2, blocks + 2, BLOCK, model_width), near_ids)]
    for bit_index in range(bit_total):
        band_tiles = shaped[:, :, bit_index % 2]
        distance = 1 << bit_index
        earlier = from_behind(band_tiles, "tm", distance)
        later = from_behind(band_tiles, "tm", -distance)
        for arrived, partner_frame in (
            (earlier, frame_index - distance),
            (later, frame_index + distance),
        ):
            frame_ok = (partner_frame >= 0) & (partner_frame < tm_count)
            ids_here = (
                partner_frame * frame_blocks + slab_index * blocks + picks_base + bit_index % 2
            )
            groups.append((arrived, jnp.where(frame_ok, ids_here, -1)))
    entry_live = jnp.arange(list_width, dtype=jnp.int32)[None, :] < block_count[:, None]
    candidates = jnp.concatenate([tiles for tiles, ids_group in groups], axis=1)
    cand_ids = jnp.concatenate([ids_group for tiles, ids_group in groups])
    cand_total = candidates.shape[1]
    flat_keys = candidates[0].reshape(cand_total * BLOCK, model_width)
    flat_values = candidates[1].reshape(cand_total * BLOCK, model_width)
    matches = block_list[:, :, None] == cand_ids[None, None, :]
    live_mask = jnp.any(matches & entry_live[:, :, None], axis=1)[:, None, :, None]

    def head_dense(head_index):
        query_head = lax.dynamic_slice_in_dim(queries, head_index * HEAD, HEAD, 1)
        key_head = lax.dynamic_slice_in_dim(flat_keys, head_index * HEAD, HEAD, 1)
        value_head = lax.dynamic_slice_in_dim(flat_values, head_index * HEAD, HEAD, 1)
        scores = (
            jnp.einsum("qd,kd->qk", query_head, key_head, preferred_element_type=jnp.float32)
            * inv_root
        )
        scores = scores.reshape(blocks, BLOCK, cand_total, BLOCK)
        masked = jnp.where(live_mask, scores, -1e30)
        row_max = jnp.max(masked, axis=(2, 3), keepdims=True)
        weights = jnp.where(live_mask, jnp.exp(masked - row_max), 0.0)
        row_sum = jnp.sum(weights, axis=(2, 3)).reshape(row_count, 1)
        rounded = weights.astype(jnp.bfloat16).reshape(row_count, cand_total * BLOCK)
        mixed_out = jnp.dot(rounded, value_head, preferred_element_type=jnp.float32)
        return (mixed_out / row_sum).astype(jnp.bfloat16)

    per_head = lax.map(head_dense, jnp.arange(head_count, dtype=jnp.int32))
    return jnp.transpose(per_head, (1, 0, 2)).reshape(row_count, model_width)


def solution(mesh):
    placed = (
        P(("tm", "space"), None),
        P(("tm", "space"), None),
        P(("tm", "space"), None),
        P(("tm", "space"), None),
        P(("tm", "space")),
    )
    return jax.shard_map(
        shards, mesh=mesh, in_specs=placed, out_specs=P(("tm", "space"), None), check_vma=False
    )
```

profile of v0, /device:TPU:18, one launch (start us, length us, event | category | flops | bytes accessed | tf_op | source)
XLA Modules:
  0.0 236.0 jit_solution(1337274853706783993)
XLA Ops:
  0.0 3.9 %fusion.24 = (bf16[2,2,128,1536]{3,2,1,0:T(8,128)(2,1)}, bf16[2,2,128,1536]{3,2,1,0:T(8,128)(2,1)}) fusion(bf16[1,2,2,128,1536]{4,3,2,1,0:T(8,128)(2,1)} %bitcast.44, bf16[1,2,2,128,1536]{4,3,2,1,0:T(8,128)(2,1)} %bitcast.47), kind=kLoop, calls=%fused_computation.25 | loop fusion | flops 1572864 | bytes 6291456 | tf_op jit(solution)/shard_map/squeeze | solution.py:57
  6.0 3.6 %collective-permute-start.3 = (bf16[2,2,128,1536]{3,2,1,0:T(8,128)(2,1)}, bf16[2,2,128,1536]{3,2,1,0:T(8,128)(2,1)}, u32[]{:S(2)}, u32[]{:S(2)}) collective-permute-start(bf16[2,2,128,1536]{3,2,1,0:T(8,128)(2,1)} %get-tuple-element.62), channel_id=1, source_target_pairs={{4,0},{8,4},{12,8},{16,12},{20,16},{24,20},{28,24},{5,1},{9,5},{13... | collective-permute-start | bytes 4718600 | tf_op jit(solution)/shard_map/ppermute | solution.py:30
  11.0 3.5 %collective-permute-start = (bf16[2,128,1536]{2,1,0:T(8,128)(2,1)}, bf16[2,128,1536]{2,1,0:T(8,128)(2,1)}, u32[]{:S(2)}, u32[]{:S(2)}) collective-permute-start(bf16[2,128,1536]{2,1,0:T(8,128)(2,1)} %get-tuple-element.63), channel_id=1, source_target_pairs={{0,1},{1,2},{2,3},{4,5},{5,6},{6,7},{8,9},{9,10},{10,11},{12,13},{... | collective-permute-start | bytes 2359304 | tf_op jit(solution)/shard_map/ppermute | solution.py:18
  14.5 2.4 collective-permute-start.1
  16.8 4.3 %collective-permute-start.4 = (bf16[2,2,128,1536]{3,2,1,0:T(8,128)(2,1)}, bf16[2,2,128,1536]{3,2,1,0:T(8,128)(2,1)}, u32[]{:S(2)}, u32[]{:S(2)}) collective-permute-start(bf16[2,2,128,1536]{3,2,1,0:T(8,128)(2,1)} %get-tuple-element.61), channel_id=1, source_target_pairs={{0,8},{4,12},{8,16},{12,20},{16,24},{20,28},{1,9},{5,13},{9,17},{1... | collective-permute-start | bytes 4718600 | tf_op jit(solution)/shard_map/ppermute | solution.py:30
  21.5 11.0 %collective-permute-done = bf16[2,128,1536]{2,1,0:T(8,128)(2,1)} collective-permute-done((bf16[2,128,1536]{2,1,0:T(8,128)(2,1)}, bf16[2,128,1536]{2,1,0:T(8,128)(2,1)}, u32[]{:S(2)}, u32[]{:S(2)}) %collective-permute-start) | collective-permute-done | bytes 786464 | tf_op jit(solution)/shard_map/ppermute | solution.py:18
  35.7 3.6 %collective-permute-start.6 = (bf16[2,2,128,1536]{3,2,1,0:T(8,128)(2,1)}, bf16[2,2,128,1536]{3,2,1,0:T(8,128)(2,1)S(1)}, u32[]{:S(2)}, u32[]{:S(2)}) collective-permute-start(bf16[2,2,128,1536]{3,2,1,0:T(8,128)(2,1)} %get-tuple-element.62), channel_id=1, source_target_pairs={{0,16},{4,20},{8,24},{12,28},{1,17},{5,21},{9,25},{13,29},{2,18},{... | collective-permute-start | bytes 4718600 | tf_op jit(solution)/shard_map/ppermute | solution.py:30
  46.2 32.2 %collective-permute-done.4 = bf16[2,2,128,1536]{3,2,1,0:T(8,128)(2,1)} collective-permute-done((bf16[2,2,128,1536]{3,2,1,0:T(8,128)(2,1)}, bf16[2,2,128,1536]{3,2,1,0:T(8,128)(2,1)}, u32[]{:S(2)}, u32[]{:S(2)}) %collective-permute-start.4) | collective-permute-done | bytes 1572896 | tf_op jit(solution)/shard_map/ppermute | solution.py:30
  80.0 31.3 %collective-permute-done.5 = bf16[2,2,128,1536]{3,2,1,0:T(8,128)(2,1)S(1)} collective-permute-done((bf16[2,2,128,1536]{3,2,1,0:T(8,128)(2,1)}, bf16[2,2,128,1536]{3,2,1,0:T(8,128)(2,1)S(1)}, u32[]{:S(2)}, u32[]{:S(2)}) %collective-permute-start.5) | collective-permute-done | bytes 1572896 | tf_op jit(solution)/shard_map/ppermute | solution.py:30
  113.3 5.3 %fusion.26 = (bf16[1,18,128,1536]{3,2,1,0:T(8,128)(2,1)}, bf16[1,18,128,1536]{3,2,1,0:T(8,128)(2,1)}) fusion(bf16[2,18,128,1536]{3,2,1,0:T(8,128)(2,1)S(1)} %constant_dynamic-update-slice_fusion.1), kind=kLoop, calls=%fused_computation.46 | loop fusion | bytes 28311552 | tf_op jit(solution)/shard_map/slice | solution.py:75
  118.6 115.9 %while.10 = (s32[]{:T(128)}, bf16[12,512,128]{1,2,0:T(8,128)(2,1)S(1)}, pred[4,1,18,1]{2,0,3,1:T(4,128)(4,1)S(1)}, s32[12]{0:T(128)S(1)}, bf16[512,1536]{1,0:T(8...) while((s32[]{:T(128)}, ...), condition=%wide.region_4.5_spmd, body=%wide.region_1.4_spmd.sunk | while | flops 614726656 | bytes 25570696 | solution.py:96
  122.5 2.2 fusion.34
  125.9 2.1 fusion.36
  132.1 2.2 fusion.34
  135.6 2.1 fusion.36
  141.8 2.2 fusion.34
  145.3 2.1 fusion.36
  151.5 2.2 fusion.34
  154.9 2.1 fusion.36
  161.1 2.2 fusion.34
  164.6 2.1 fusion.36
  170.8 2.2 fusion.34
  174.2 2.1 fusion.36
  180.4 2.2 fusion.34
  183.9 2.1 fusion.36
  190.1 2.2 fusion.34
  193.6 2.1 fusion.36
  199.8 2.2 fusion.34
  203.2 2.1 fusion.36
  209.4 2.2 fusion.34
  219.1 2.2 fusion.34
  228.7 2.2 fusion.34
  (136 shorter events, 80.2 us)
Async XLA Ops:
  0.0 9.6 %copy-start = (bf16[512,1536]{1,0:T(8,128)(2,1)S(1)}, bf16[512,1536]{1,0:T(8,128)(2,1)}, u32[]{:S(2)}) copy-start(bf16[512,1536]{1,0:T(8,128)(2,1)} %param.9) | copy-start | bytes 4718596
  0.0 9.6 %copy-start.1 = (bf16[512,1536]{1,0:T(8,128)(2,1)S(1)}, bf16[512,1536]{1,0:T(8,128)(2,1)}, u32[]{:S(2)}) copy-start(bf16[512,1536]{1,0:T(8,128)(2,1)} %param.8) | copy-start | bytes 4718596
  3.9 17.4 %copy-start.4 = (s32[4]{0:T(128)S(1)}, s32[4]{0:T(128)}, u32[]{:S(2)}) copy-start(s32[4]{0:T(128)} %param.11) | copy-start | bytes 52
  3.9 17.5 %copy-start.3 = (s32[4,8]{1,0:T(4,128)S(1)}, s32[4,8]{1,0:T(4,128)}, u32[]{:S(2)}) copy-start(s32[4,8]{1,0:T(4,128)} %param.10) | copy-start | bytes 388
  3.9 36.9 %collective-permute-start.2 = (bf16[2,2,128,1536]{3,2,1,0:T(8,128)(2,1)}, bf16[2,2,128,1536]{3,2,1,0:T(8,128)(2,1)}, u32[]{:S(2)}, u32[]{:S(2)}) collective-permute-start(bf16[2,2,128,1536]{3,2,1,0:T(8,128)(2,1)} %get-tuple-element.62), channel_id=1, source_target_pairs={{0,4},{4,8},{8,12},{12,16},{16,20},{20,24},{24,28},{1,5},{5,9},{9,... | collective-permute-start | bytes 4718600 | tf_op jit(solution)/shard_map/ppermute | solution.py:30
  6.0 38.7 %collective-permute-start.3 = (bf16[2,2,128,1536]{3,2,1,0:T(8,128)(2,1)}, bf16[2,2,128,1536]{3,2,1,0:T(8,128)(2,1)}, u32[]{:S(2)}, u32[]{:S(2)}) collective-permute-start(bf16[2,2,128,1536]{3,2,1,0:T(8,128)(2,1)} %get-tuple-element.62), channel_id=1, source_target_pairs={{4,0},{8,4},{12,8},{16,12},{20,16},{24,20},{28,24},{5,1},{9,5},{13... | collective-permute-start | bytes 4718600 | tf_op jit(solution)/shard_map/ppermute | solution.py:30
  11.0 21.5 %collective-permute-start = (bf16[2,128,1536]{2,1,0:T(8,128)(2,1)}, bf16[2,128,1536]{2,1,0:T(8,128)(2,1)}, u32[]{:S(2)}, u32[]{:S(2)}) collective-permute-start(bf16[2,128,1536]{2,1,0:T(8,128)(2,1)} %get-tuple-element.63), channel_id=1, source_target_pairs={{0,1},{1,2},{2,3},{4,5},{5,6},{6,7},{8,9},{9,10},{10,11},{12,13},{... | collective-permute-start | bytes 2359304 | tf_op jit(solution)/shard_map/ppermute | solution.py:18
  14.5 21.2 %collective-permute-start.1 = (bf16[2,128,1536]{2,1,0:T(8,128)(2,1)}, bf16[2,128,1536]{2,1,0:T(8,128)(2,1)}, u32[]{:S(2)}, u32[]{:S(2)}) collective-permute-start(bf16[2,128,1536]{2,1,0:T(8,128)(2,1)} %get-tuple-element.64), channel_id=1, source_target_pairs={{1,0},{2,1},{3,2},{5,4},{6,5},{7,6},{9,8},{10,9},{11,10},{13,12},{... | collective-permute-start | bytes 2359304 | tf_op jit(solution)/shard_map/ppermute | solution.py:20
  16.8 61.6 %collective-permute-start.4 = (bf16[2,2,128,1536]{3,2,1,0:T(8,128)(2,1)}, bf16[2,2,128,1536]{3,2,1,0:T(8,128)(2,1)}, u32[]{:S(2)}, u32[]{:S(2)}) collective-permute-start(bf16[2,2,128,1536]{3,2,1,0:T(8,128)(2,1)} %get-tuple-element.61), channel_id=1, source_target_pairs={{0,8},{4,12},{8,16},{12,20},{16,24},{20,28},{1,9},{5,13},{9,17},{1... | collective-permute-start | bytes 4718600 | tf_op jit(solution)/shard_map/ppermute | solution.py:30
  32.5 78.8 %collective-permute-start.5 = (bf16[2,2,128,1536]{3,2,1,0:T(8,128)(2,1)}, bf16[2,2,128,1536]{3,2,1,0:T(8,128)(2,1)S(1)}, u32[]{:S(2)}, u32[]{:S(2)}) collective-permute-start(bf16[2,2,128,1536]{3,2,1,0:T(8,128)(2,1)} %get-tuple-element.61), channel_id=1, source_target_pairs={{8,0},{12,4},{16,8},{20,12},{24,16},{28,20},{9,1},{13,5},{17,9},{2... | collective-permute-start | bytes 4718600 | tf_op jit(solution)/shard_map/ppermute | solution.py:30
  35.7 75.7 %collective-permute-start.6 = (bf16[2,2,128,1536]{3,2,1,0:T(8,128)(2,1)}, bf16[2,2,128,1536]{3,2,1,0:T(8,128)(2,1)S(1)}, u32[]{:S(2)}, u32[]{:S(2)}) collective-permute-start(bf16[2,2,128,1536]{3,2,1,0:T(8,128)(2,1)} %get-tuple-element.62), channel_id=1, source_target_pairs={{0,16},{4,20},{8,24},{12,28},{1,17},{5,21},{9,25},{13,29},{2,18},{... | collective-permute-start | bytes 4718600 | tf_op jit(solution)/shard_map/ppermute | solution.py:30
  40.9 72.3 %collective-permute-start.7 = (bf16[2,2,128,1536]{3,2,1,0:T(8,128)(2,1)}, bf16[2,2,128,1536]{3,2,1,0:T(8,128)(2,1)S(1)}, u32[]{:S(2)}, u32[]{:S(2)}) collective-permute-start(bf16[2,2,128,1536]{3,2,1,0:T(8,128)(2,1)} %get-tuple-element.62), channel_id=1, source_target_pairs={{16,0},{20,4},{24,8},{28,12},{17,1},{21,5},{25,9},{29,13},{18,2},{... | collective-permute-start | bytes 4718600 | tf_op jit(solution)/shard_map/ppermute | solution.py:30
  113.3 5.3 %copy-start.2 = (bf16[12,512,128]{1,2,0:T(8,128)(2,1)S(1)}, bf16[12,512,128]{1,2,0:T(8,128)(2,1)}, u32[]{:S(2)}) copy-start(bf16[12,512,128]{1,2,0:T(8,128)(2,1)} %custom-call.1) | copy-start | bytes 4718596
where the time goes:
time: 238 us; the launch traced here: 236 us
  waiting for transfers between devices  78.2 us (33%)
  local copies, waits for them, and re-layouts  52.5 us (22%)
  matrix products  52.3 us (22%)
  starting transfers between devices  22.6 us (9%)
  other arithmetic  21.6 us (9%)
  loops' own time  8.6 us (4%)
    ppermute x6, waiting for transfers between devices, from_behind(): return lax.ppermute(shard, axis, pairs)  65.9 us
    dot_general x12, matrix products, head_dense(): jnp.einsum('qd,kd->qk', query_head, key_head, preferred_element_type=jnp....  26.8 us
    dot_general x12, matrix products, head_dense(): mixed_out = jnp.dot(rounded, value_head, preferred_element_type=jnp.float32)  25.5 us
    broadcast_in_dim x36, local copies, waits for them, and re-layouts, head_dense(): weights = jnp.where(live_mask, jnp.exp(masked - row_max), 0.0)  25 us
    ppermute x6, starting transfers between devices, from_behind(): return lax.ppermute(shard, axis, pairs)  16.7 us
    reduce_sum x12, other arithmetic, head_dense(): row_sum = jnp.sum(weights, axis=(2, 3)).reshape(row_count, 1)  14.6 us
    ppermute x1, waiting for transfers between devices, with_halo(): lax.ppermute(tail, axis, [(i, (i + 1) % count) for i in range(ends)])  11 us
    another operation x1, loops' own time, shards(): per_head = lax.map(head_dense, jnp.arange(head_count, dtype=jnp.int32))  8.6 us
  transfers between devices with their start and end apart: 8, of which 6 were waited for; matrix products, arithmetic and copies ran while one was open for 3% of the time, Pallas kernels for 0%

commit v1 on v0

v1 whole, which is shorter than its diff:
```python
import functools
import math

import jax
import jax.numpy as jnp
from jax import lax
from jax.experimental import pallas as pl
from jax.experimental.pallas import tpu as pltpu
from jax.sharding import PartitionSpec as P

HEAD = 128
BLOCK = 128
DEAD = -1e30
MESH = pl.DeviceIdType.MESH


def kernel(
    tm_count, space_count, list_width,
    q_hbm, k_hbm, v_hbm, list_ref, count_ref, o_ref,
    q_own, k_own, v_own, k_halo, v_halo, k_band, v_band,
    top, total, mixed, near_bias, band_bias,
    local_sem, halo_send, halo_recv, band_send, band_recv, relay_send,
):
    rows, width = q_hbm.shape
    blocks = rows // BLOCK
    picks = blocks // 2
    heads = width // HEAD
    bits = tm_count.bit_length() - 1
    half = tm_count // 2
    relayed = bits == 3
    frame = lax.axis_index("tm")
    slab = lax.axis_index("space")
    scale = math.log2(math.e) / HEAD**0.5

    def flag(pred):
        return jnp.where(pred, 1, 0)

    def exists(delta):
        return (frame + delta >= 0) & (frame + delta < tm_count)

    def slab_exists(delta):
        return (slab + delta >= 0) & (slab + delta < space_count)

    barrier = pltpu.get_barrier_semaphore()
    greets = []
    for delta in (-1, 1):
        greets.append((slab_exists(delta), {"space": slab + delta}))
    for bit in range(bits):
        for delta in (-(1 << bit), 1 << bit):
            greets.append((exists(delta), {"tm": frame + delta}))
    if relayed:
        greets.append((frame == 0, {"tm": frame + half - 1}))
        greets.append((frame == half - 1, {"tm": frame - half + 1}))
        greets.append((frame == tm_count - 1, {"tm": frame - half + 1}))
        greets.append((frame == half, {"tm": frame + half - 1}))
    expected = 0
    for pred, device in greets:
        expected = expected + flag(pred)

        @pl.when(pred)
        def _(device=device):
            pl.semaphore_signal(barrier, inc=1, device_id=device, device_id_type=MESH)

    pl.semaphore_wait(barrier, expected)

    def halo_copies(side, delta):
        start = (blocks - 1) * BLOCK if side == 0 else 0
        for index, (src, dst) in enumerate(((k_hbm, k_halo), (v_hbm, v_halo))):
            yield pltpu.make_async_remote_copy(
                src_ref=src.at[pl.ds(start, BLOCK)],
                dst_ref=dst.at[side],
                send_sem=halo_send.at[side, index],
                recv_sem=halo_recv.at[side, index],
                device_id={"space": slab + delta},
                device_id_type=MESH,
            )

    def band_copy(bit, side, chunk, device):
        pick, which = chunk // 2, chunk % 2
        src = (k_hbm, v_hbm)[which]
        dst = (k_band, v_band)[which]
        slot = 2 * bit + side
        return pltpu.make_async_remote_copy(
            src_ref=src.at[pl.ds((2 * pick + bit % 2) * BLOCK, BLOCK)],
            dst_ref=dst.at[slot, pl.ds(pick * BLOCK, BLOCK)],
            send_sem=band_send.at[slot, chunk],
            recv_sem=band_recv.at[slot, chunk],
            device_id={"tm": device},
            device_id_type=MESH,
        )

    def relay_copy(kind, slot_from, slot_to, chunk, device):
        pick, which = chunk // 2, chunk % 2
        buf = (k_band, v_band)[which]
        return pltpu.make_async_remote_copy(
            src_ref=buf.at[slot_from, pl.ds(pick * BLOCK, BLOCK)],
            dst_ref=buf.at[slot_to, pl.ds(pick * BLOCK, BLOCK)],
            send_sem=relay_send.at[kind, chunk],
            recv_sem=band_recv.at[slot_to, chunk],
            device_id={"tm": device},
            device_id_type=MESH,
        )

    def sends(bit, side):
        delta = (1 << bit) if side == 0 else -(1 << bit)
        pred = exists(delta)
        if relayed and bit == 0:
            pred = pred & (frame != (half - 1 if side == 0 else half))
        if relayed and bit == 1:
            if side == 0:
                pred = pred & ((frame < half - 2) | (frame >= half))
            else:
                pred = pred & ((frame < half) | (frame >= half + 2))
        return pred, frame + delta

    chunks = 2 * picks
    for side, delta in ((0, 1), (1, -1)):

        @pl.when(slab_exists(delta))
        def _(side=side, delta=delta):
            for copy in halo_copies(side, delta):
                copy.start()

    order = list(range(1, bits)) + [0]
    for chunk in range(chunks):
        for bit in order:
            for side in (0, 1):
                pred, device = sends(bit, side)

                @pl.when(pred)
                def _(bit=bit, side=side, chunk=chunk, device=device):
                    band_copy(bit, side, chunk, device).start()

    local = [
        pltpu.make_async_copy(src, dst, local_sem.at[index])
        for index, (src, dst) in enumerate(((q_hbm, q_own), (k_hbm, k_own), (v_hbm, v_own)))
    ]
    for copy in local:
        copy.start()

    frame_blocks = blocks * space_count
    first_block = frame * frame_blocks + slab * blocks

    def bias_rows(ids):
        row = jnp.concatenate([jnp.full((1, BLOCK), ident, jnp.int32) for ident in ids], axis=1)
        out = []
        for tile in range(blocks):
            count = count_ref[tile]
            value = jnp.full(row.shape, DEAD, jnp.float32)
            for entry in range(list_width):
                listed = jnp.where(entry < count, list_ref[tile, entry], -1)
                value = jnp.where(row == listed, 0.0, value)
            out.append(value)
        return out

    near_ids = [first_block + c for c in range(blocks)] + [first_block - 1, first_block + blocks]
    for tile, value in enumerate(bias_rows(near_ids)):
        near_bias[tile : tile + 1, :] = value
    for bit in range(bits):
        for side in (0, 1):
            partner = frame - (1 << bit) if side == 0 else frame + (1 << bit)
            ids = [
                partner * frame_blocks + slab * blocks + 2 * pick + bit % 2
                for pick in range(picks)
            ]
            for tile, value in enumerate(bias_rows(ids)):
                band_bias[2 * bit + side, tile : tile + 1, :] = value

    for copy in local:
        copy.wait()

    def attend(get_k, get_v, get_bias, keys, first):
        ones = jnp.ones((keys, HEAD), jnp.bfloat16)

        def one_head(head, carry):
            cols = pl.ds(pl.multiple_of(head * HEAD, HEAD), HEAD)
            raw = lax.dot_general(
                q_own[:, cols], get_k(cols), (((1,), (1,)), ((), ())),
                preferred_element_type=jnp.float32,
            )
            parts, shrink = [], []
            for tile in range(blocks):
                span = slice(tile * BLOCK, (tile + 1) * BLOCK)
                scores = raw[span] * scale + get_bias(tile)
                peak = jnp.max(scores, axis=1, keepdims=True)
                if first:
                    new_top = jnp.broadcast_to(peak, (BLOCK, HEAD))
                else:
                    old_top = top[head, span, :]
                    new_top = jnp.maximum(old_top, peak)
                    shrink.append(jnp.exp2(old_top - new_top))
                top[head, span, :] = new_top
                wide = jnp.concatenate([new_top] * (keys // HEAD), axis=1)
                parts.append(jnp.exp2(scores - wide).astype(jnp.bfloat16))
            weights = jnp.concatenate(parts, axis=0)
            extended = jnp.concatenate([get_v(cols), ones], axis=1)
            both = jnp.dot(weights, extended, preferred_element_type=jnp.float32)
            if first:
                mixed[head] = both[:, :HEAD]
                total[head] = both[:, HEAD:]
            else:
                factor = jnp.concatenate(shrink, axis=0)
                mixed[head] = mixed[head] * factor + both[:, :HEAD]
                total[head] = total[head] * factor + both[:, HEAD:]
            return carry

        lax.fori_loop(0, heads, one_head, 0)

    attend(
        lambda cols: k_own[:, cols],
        lambda cols: v_own[:, cols],
        lambda tile: near_bias[tile : tile + 1, : blocks * BLOCK],
        blocks * BLOCK,
        True,
    )

    def halo(side, delta):
        @pl.when(slab_exists(delta))
        def _():
            for copy in halo_copies(side, delta):
                copy.wait_recv()
            start = (blocks + side) * BLOCK
            attend(
                lambda cols: k_halo[side, :, cols],
                lambda cols: v_halo[side, :, cols],
                lambda tile: near_bias[tile : tile + 1, start : start + BLOCK],
                BLOCK,
                False,
            )

    halo(0, -1)
    halo(1, 1)

    def band_wait(bit, side, chunk):
        slot = 2 * bit + side
        pick, which = chunk // 2, chunk % 2
        buf = (k_band, v_band)[which]
        pltpu.make_async_remote_copy(
            src_ref=(k_hbm, v_hbm)[which].at[pl.ds(0, BLOCK)],
            dst_ref=buf.at[slot, pl.ds(pick * BLOCK, BLOCK)],
            send_sem=band_send.at[slot, chunk],
            recv_sem=band_recv.at[slot, chunk],
            device_id={"tm": frame},
            device_id_type=MESH,
        ).wait_recv()

    early = frame < half
    outer = (frame < 2) | (frame >= tm_count - 2)
    corner = (frame == 0) | (frame == tm_count - 1)
    inward = flag(early)
    last = bits - 1
    relay_pair = (
        (outer, lambda chunk: relay_copy(
            0, 2 + inward, 3 - inward, chunk, jnp.where(early, frame + half, frame - half))),
        (corner, lambda chunk: relay_copy(
            1, 2 * last + inward, inward, chunk, jnp.where(early, half - 1, half))),
    )
    if relayed:
        for chunk in range(chunks):
            for (pred, make), bit in zip(relay_pair, (1, last)):

                @pl.when(pred)
                def _(make=make, bit=bit, chunk=chunk):
                    band_wait(bit, inward, chunk)
                    make(chunk).start()

    def band(bit, side, waited):
        delta = jnp.where(side == 0, -(1 << bit), 1 << bit)

        @pl.when(exists(delta))
        def _():
            @pl.when(jnp.logical_not(waited))
            def _():
                for chunk in range(chunks):
                    band_wait(bit, side, chunk)

            slot = 2 * bit + side
            attend(
                lambda cols: k_band[slot, :, cols],
                lambda cols: v_band[slot, :, cols],
                lambda tile: band_bias[slot, tile : tile + 1, :],
                picks * BLOCK,
                False,
            )

    never = frame < 0
    other = 1 - inward
    core_side = 1 - lax.rem(frame, 2)
    relay_b = outer if relayed else never
    relay_a = corner if relayed else never
    band(0, core_side, never)
    for bit in range(2, bits - 1):
        band(bit, other, never)
        band(bit, inward, never)
    band(last, inward, relay_a)
    if bits > 1:
        band(1, other, never)
    band(0, 1 - core_side, never)
    if bits > 1:
        band(1, inward, relay_b)

    def finish(head, carry):
        cols = pl.ds(pl.multiple_of(head * HEAD, HEAD), HEAD)
        o_ref[:, cols] = (mixed[head] / total[head]).astype(o_ref.dtype)
        return carry

    lax.fori_loop(0, heads, finish, 0)

    for side, delta in ((0, 1), (1, -1)):

        @pl.when(slab_exists(delta))
        def _(side=side, delta=delta):
            for copy in halo_copies(side, delta):
                copy.wait_send()

    for bit in range(bits):
        for side in (0, 1):
            pred, device = sends(bit, side)

            @pl.when(pred)
            def _(bit=bit, side=side, device=device):
                for chunk in range(chunks):
                    band_copy(bit, side, chunk, device).wait_send()

    if relayed:
        for pred, make in relay_pair:

            @pl.when(pred)
            def _(make=make):
                for chunk in range(chunks):
                    make(chunk).wait_send()


def shards(tm_count, space_count, queries, key_rows, value_rows, block_list, block_count):
    rows, width = queries.shape
    blocks = rows // BLOCK
    picks = blocks // 2
    heads = width // HEAD
    slots = 2 * (tm_count.bit_length() - 1)
    kind = key_rows.dtype
    anywhere = pl.BlockSpec(memory_space=pl.ANY)
    scalar = pl.BlockSpec(memory_space=pltpu.SMEM)
    dma = pltpu.SemaphoreType.DMA
    return pl.pallas_call(
        functools.partial(kernel, tm_count, space_count, block_list.shape[1]),
        out_shape=jax.ShapeDtypeStruct((rows, width), queries.dtype),
        in_specs=[anywhere, anywhere, anywhere, scalar, scalar],
        out_specs=pl.BlockSpec(memory_space=pltpu.VMEM),
        scratch_shapes=[
            pltpu.VMEM((rows, width), kind),
            pltpu.VMEM((rows, width), kind),
            pltpu.VMEM((rows, width), kind),
            pltpu.VMEM((2, BLOCK, width), kind),
            pltpu.VMEM((2, BLOCK, width), kind),
            pltpu.VMEM((slots, picks * BLOCK, width), kind),
            pltpu.VMEM((slots, picks * BLOCK, width), kind),
            pltpu.VMEM((heads, rows, HEAD), jnp.float32),
            pltpu.VMEM((heads, rows, HEAD), jnp.float32),
            pltpu.VMEM((heads, rows, HEAD), jnp.float32),
            pltpu.VMEM((blocks, (blocks + 2) * BLOCK), jnp.float32),
            pltpu.VMEM((slots, blocks, picks * BLOCK), jnp.float32),
            dma((3,)),
            dma((2, 2)),
            dma((2, 2)),
            dma((slots, 2 * picks)),
            dma((slots, 2 * picks)),
            dma((2, 2 * picks)),
        ],
        compiler_params=pltpu.CompilerParams(
            collective_id=0, has_side_effects=True, vmem_limit_bytes=60 * 1024 * 1024
        ),
    )(queries, key_rows, value_rows, block_list, block_count)


def solution(mesh):
    placed = (
        P(("tm", "space"), None),
        P(("tm", "space"), None),
        P(("tm", "space"), None),
        P(("tm", "space"), None),
        P(("tm", "space")),
    )
    return jax.shard_map(
        functools.partial(shards, mesh.shape["tm"], mesh.shape["space"]),
        mesh=mesh, in_specs=placed, out_specs=P(("tm", "space"), None), check_vma=False,
    )
```

time: 238 us -> 88.8 us (0.37)
  Pallas kernels: 0 us -> 84.9 us
  waiting for transfers between devices: 78.2 us -> 0 us
  matrix products: 52.3 us -> 0 us
  local copies, waits for them, and re-layouts: 52.5 us -> 2.65 us
  starting transfers between devices: 22.6 us -> 0 us
  other arithmetic: 21.6 us -> 0 us
  loops' own time: 8.6 us -> 0 us
    pallas_call x0 -> x1, Pallas kernels: none -> 84.9 us  [shards(): pl.pallas_call(functools.partial(kernel, tm_count, space_count, block_lis...]
    ppermute x8 -> x0, waiting for transfers between devices: 78.2 us -> none  [the longest x6 65.9 us: from_behind(): return lax.ppermute(shard, axis, pairs)]
    dot_general x24 -> x0, matrix products: 52.3 us -> none  [the longest x12 26.8 us: head_dense(): jnp.einsum('qd,kd->qk', query_head, key_head, preferred_element_type=jnp....]
    broadcast_in_dim x36 -> x0, local copies, waits for them, and re-layouts: 25 us -> none  [head_dense(): weights = jnp.where(live_mask, jnp.exp(masked - row_max), 0.0)]
    ppermute x8 -> x0, starting transfers between devices: 22.6 us -> none  [the longest x6 16.7 us: from_behind(): return lax.ppermute(shard, axis, pairs)]
    reduce_sum x12 -> x0, other arithmetic: 14.6 us -> none  [head_dense(): row_sum = jnp.sum(weights, axis=(2, 3)).reshape(row_count, 1)]
    another operation x1 -> x0, loops' own time: 8.6 us -> none  [shards(): per_head = lax.map(head_dense, jnp.arange(head_count, dtype=jnp.int32))]
    dynamic_slice x12 -> x0, local copies, waits for them, and re-layouts: 7.03 us -> none  [shards(): per_head = lax.map(head_dense, jnp.arange(head_count, dtype=jnp.int32))]
  transfers between devices with their start and end apart: 8 -> 0, of which waited for: 6 -> 0; matrix products, arithmetic and copies ran while one was open for 3% -> 0% of each run, Pallas kernels for 0% -> 0%
where the time goes in v1:
time: 88.8 us; the launch traced here: 87.6 us
  Pallas kernels  84.9 us (96%)
  local copies, waits for them, and re-layouts  2.65 us (3%)
    pallas_call x1, Pallas kernels, shards(): pl.pallas_call(functools.partial(kernel, tm_count, space_count, block_lis...  84.9 us
    unnamed x1, local copies, waits for them, and re-layouts  2.65 us

profile of v1, /device:TPU:18, one launch (start us, length us, event | category | flops | bytes accessed | tf_op | source)
XLA Modules:
  0.0 87.6 jit_solution(9038370851904179037)
XLA Ops:
  0.0 84.9 %shard_map.55 = bf16[512,1536]{1,0:T(8,128)(2,1)} custom-call(bf16[512,1536]{1,0:T(8,128)(2,1)} %q_hbm.1, bf16[512,1536]{1,0:T(8,128)(2,1)} %k_hbm.1, bf16[512,1536]{1,0:T(8,128)(2,1)} %v_hbm.1, s32[4,8]{1,0:T(4,128)} %list_ref.1, s32[4]{0:T(128)} %count_ref.1), custom_call_target="tpu_custom_call" | custom-call | tf_op jit(solution)/shard_map/pallas_call | solution.py:344
  84.9 2.7 %copy.7 = bf16[512,1536]{1,0:T(8,128)(2,1)} copy(bf16[512,1536]{1,0:T(8,128)(2,1)} %shard_map.55) | data formatting | bytes 3145728

commit v2 on v1

--- a/solution.py
+++ b/solution.py
@@ -15,7 +15,7 @@
 
 
 def kernel(
-    tm_count, space_count, list_width,
+    tm_count, space_count, list_width, parts,
     q_hbm, k_hbm, v_hbm, list_ref, count_ref, o_ref,
     q_own, k_own, v_own, k_halo, v_halo, k_band, v_band,
     top, total, mixed, near_bias, band_bias,
@@ -75,31 +75,33 @@
                 device_id_type=MESH,
             )
 
-    def band_copy(bit, side, chunk, device):
-        pick, which = chunk // 2, chunk % 2
-        src = (k_hbm, v_hbm)[which]
-        dst = (k_band, v_band)[which]
+    part_width = width // parts
+
+    def part_cols(part):
+        return pl.ds(pl.multiple_of(part * part_width, part_width), part_width)
+
+    def band_copies(bit, side, part, device):
         slot = 2 * bit + side
-        return pltpu.make_async_remote_copy(
-            src_ref=src.at[pl.ds((2 * pick + bit % 2) * BLOCK, BLOCK)],
-            dst_ref=dst.at[slot, pl.ds(pick * BLOCK, BLOCK)],
-            send_sem=band_send.at[slot, chunk],
-            recv_sem=band_recv.at[slot, chunk],
-            device_id={"tm": device},
-            device_id_type=MESH,
-        )
-
-    def relay_copy(kind, slot_from, slot_to, chunk, device):
-        pick, which = chunk // 2, chunk % 2
-        buf = (k_band, v_band)[which]
-        return pltpu.make_async_remote_copy(
-            src_ref=buf.at[slot_from, pl.ds(pick * BLOCK, BLOCK)],
-            dst_ref=buf.at[slot_to, pl.ds(pick * BLOCK, BLOCK)],
-            send_sem=relay_send.at[kind, chunk],
-            recv_sem=band_recv.at[slot_to, chunk],
-            device_id={"tm": device},
-            device_id_type=MESH,
-        )
+        for which, (src, dst) in enumerate(((k_hbm, k_band), (v_hbm, v_band))):
+            yield pltpu.make_async_remote_copy(
+                src_ref=src.reshape(picks, 2, BLOCK, width).at[:, bit % 2, :, part_cols(part)],
+                dst_ref=dst.at[slot, :, :, part_cols(part)],
+                send_sem=band_send.at[slot, part, which],
+                recv_sem=band_recv.at[slot, part, which],
+                device_id={"tm": device},
+                device_id_type=MESH,
+            )
+
+    def relay_copies(kind, slot_from, slot_to, part, device):
+        for which, buf in enumerate((k_band, v_band)):
+            yield pltpu.make_async_remote_copy(
+                src_ref=buf.at[slot_from, :, :, part_cols(part)],
+                dst_ref=buf.at[slot_to, :, :, part_cols(part)],
+                send_sem=relay_send.at[kind, part, which],
+                recv_sem=band_recv.at[slot_to, part, which],
+                device_id={"tm": device},
+                device_id_type=MESH,
+            )
 
     def sends(bit, side):
         delta = (1 << bit) if side == 0 else -(1 << bit)
@@ -113,7 +115,6 @@
                 pred = pred & ((frame < half) | (frame >= half + 2))
         return pred, frame + delta
 
-    chunks = 2 * picks
     for side, delta in ((0, 1), (1, -1)):
 
         @pl.when(slab_exists(delta))
@@ -122,14 +123,15 @@
                 copy.start()
 
     order = list(range(1, bits)) + [0]
-    for chunk in range(chunks):
-        for bit in order:
-            for side in (0, 1):
-                pred, device = sends(bit, side)
-
-                @pl.when(pred)
-                def _(bit=bit, side=side, chunk=chunk, device=device):
-                    band_copy(bit, side, chunk, device).start()
+    for bit in order:
+        for side in (0, 1):
+            pred, device = sends(bit, side)
+
+            @pl.when(pred)
+            def _(bit=bit, side=side, device=device):
+                for part in range(parts):
+                    for copy in band_copies(bit, side, part, device):
+                        copy.start()
 
     local = [
         pltpu.make_async_copy(src, dst, local_sem.at[index])
@@ -169,7 +171,7 @@
     for copy in local:
         copy.wait()
 
-    def attend(get_k, get_v, get_bias, keys, first):
+    def attend(get_k, get_v, get_bias, keys, first=False, final=False, bounds=None):
         ones = jnp.ones((keys, HEAD), jnp.bfloat16)
 
         def one_head(head, carry):
@@ -189,7 +191,8 @@
                     old_top = top[head, span, :]
                     new_top = jnp.maximum(old_top, peak)
                     shrink.append(jnp.exp2(old_top - new_top))
-                top[head, span, :] = new_top
+                if not final:
+                    top[head, span, :] = new_top
                 wide = jnp.concatenate([new_top] * (keys // HEAD), axis=1)
                 parts.append(jnp.exp2(scores - wide).astype(jnp.bfloat16))
             weights = jnp.concatenate(parts, axis=0)
@@ -200,18 +203,24 @@
                 total[head] = both[:, HEAD:]
             else:
                 factor = jnp.concatenate(shrink, axis=0)
-                mixed[head] = mixed[head] * factor + both[:, :HEAD]
-                total[head] = total[head] * factor + both[:, HEAD:]
+                new_mixed = mixed[head] * factor + both[:, :HEAD]
+                new_total = total[head] * factor + both[:, HEAD:]
+                if final:
+                    o_ref[:, cols] = (new_mixed / new_total).astype(o_ref.dtype)
+                else:
+                    mixed[head] = new_mixed
+                    total[head] = new_total
             return carry
 
-        lax.fori_loop(0, heads, one_head, 0)
+        low, high = (0, heads) if bounds is None else bounds
+        lax.fori_loop(low, high, one_head, 0)
 
     attend(
         lambda cols: k_own[:, cols],
         lambda cols: v_own[:, cols],
         lambda tile: near_bias[tile : tile + 1, : blocks * BLOCK],
         blocks * BLOCK,
-        True,
+        first=True,
     )
 
     def halo(side, delta):
@@ -225,24 +234,22 @@
                 lambda cols: v_halo[side, :, cols],
                 lambda tile: near_bias[tile : tile + 1, start : start + BLOCK],
                 BLOCK,
-                False,
             )
 
     halo(0, -1)
     halo(1, 1)
 
-    def band_wait(bit, side, chunk):
+    def band_wait(bit, side, part):
         slot = 2 * bit + side
-        pick, which = chunk // 2, chunk % 2
-        buf = (k_band, v_band)[which]
-        pltpu.make_async_remote_copy(
-            src_ref=(k_hbm, v_hbm)[which].at[pl.ds(0, BLOCK)],
-            dst_ref=buf.at[slot, pl.ds(pick * BLOCK, BLOCK)],
-            send_sem=band_send.at[slot, chunk],
-            recv_sem=band_recv.at[slot, chunk],
-            device_id={"tm": frame},
-            device_id_type=MESH,
-        ).wait_recv()
+        for which, (src, dst) in enumerate(((k_hbm, k_band), (v_hbm, v_band))):
+            pltpu.make_async_remote_copy(
+                src_ref=src.reshape(picks, 2, BLOCK, width).at[:, 0, :, part_cols(part)],
+                dst_ref=dst.at[slot, :, :, part_cols(part)],
+                send_sem=band_send.at[slot, part, which],
+                recv_sem=band_recv.at[slot, part, which],
+                device_id={"tm": frame},
+                device_id_type=MESH,
+            ).wait_recv()
 
     early = frame < half
     outer = (frame < 2) | (frame >= tm_count - 2)
@@ -250,61 +257,90 @@
     inward = flag(early)
     last = bits - 1
     relay_pair = (
-        (outer, lambda chunk: relay_copy(
-            0, 2 + inward, 3 - inward, chunk, jnp.where(early, frame + half, frame - half))),
-        (corner, lambda chunk: relay_copy(
-            1, 2 * last + inward, inward, chunk, jnp.where(early, half - 1, half))),
+        (outer, lambda part: relay_copies(
+            0, 2 + inward, 3 - inward, part, jnp.where(early, frame + half, frame - half))),
+        (corner, lambda part: relay_copies(
+            1, 2 * last + inward, inward, part, jnp.where(early, half - 1, half))),
     )
     if relayed:
-        for chunk in range(chunks):
+        for part in range(parts):
             for (pred, make), bit in zip(relay_pair, (1, last)):
 
                 @pl.when(pred)
-                def _(make=make, bit=bit, chunk=chunk):
-                    band_wait(bit, inward, chunk)
-                    make(chunk).start()
+                def _(make=make, bit=bit, part=part):
+                    band_wait(bit, inward, part)
+                    for copy in make(part):
+                        copy.start()
+
+    def band_exists(bit, side):
+        return exists(jnp.where(side == 0, -(1 << bit), 1 << bit))
+
+    def band_keys(slot):
+        return (
+            lambda cols: k_band[slot, :, :, cols].reshape(picks * BLOCK, HEAD),
+            lambda cols: v_band[slot, :, :, cols].reshape(picks * BLOCK, HEAD),
+            lambda tile: band_bias[slot, tile : tile + 1, :],
+        )
 
     def band(bit, side, waited):
-        delta = jnp.where(side == 0, -(1 << bit), 1 << bit)
-
-        @pl.when(exists(delta))
+        @pl.when(band_exists(bit, side))
         def _():
             @pl.when(jnp.logical_not(waited))
             def _():
-                for chunk in range(chunks):
-                    band_wait(bit, side, chunk)
-
-            slot = 2 * bit + side
-            attend(
-                lambda cols: k_band[slot, :, cols],
-                lambda cols: v_band[slot, :, cols],
-                lambda tile: band_bias[slot, tile : tile + 1, :],
-                picks * BLOCK,
-                False,
-            )
+                for part in range(parts):
+                    band_wait(bit, side, part)
+
+            attend(*band_keys(2 * bit + side), picks * BLOCK)
 
     never = frame < 0
     other = 1 - inward
     core_side = 1 - lax.rem(frame, 2)
+    relay_a = corner if relayed else never
     relay_b = outer if relayed else never
-    relay_a = corner if relayed else never
     band(0, core_side, never)
     for bit in range(2, bits - 1):
         band(bit, other, never)
         band(bit, inward, never)
     band(last, inward, relay_a)
-    if bits > 1:
-        band(1, other, never)
-    band(0, 1 - core_side, never)
-    if bits > 1:
-        band(1, inward, relay_b)
-
-    def finish(head, carry):
-        cols = pl.ds(pl.multiple_of(head * HEAD, HEAD), HEAD)
-        o_ref[:, cols] = (mixed[head] / total[head]).astype(o_ref.dtype)
-        return carry
-
-    lax.fori_loop(0, heads, finish, 0)
+    band(1, other, never)
+
+    late = ((0, 1 - core_side, never), (1, inward, relay_b))
+    both_exist = band_exists(0, 1 - core_side) & band_exists(1, inward)
+    heads_part = heads // parts
+
+    @pl.when(both_exist)
+    def _():
+        getters = [band_keys(2 * bit + side) for bit, side, _ in late]
+
+        def joined(index, axis):
+            return lambda arg: jnp.concatenate([g[index](arg) for g in getters], axis=axis)
+
+        def one_part(part, carry):
+            for bit, side, waited in late:
+
+                @pl.when(jnp.logical_not(waited))
+                def _(bit=bit, side=side):
+                    band_wait(bit, side, part)
+
+            attend(
+                joined(0, 0), joined(1, 0), joined(2, 1), 2 * picks * BLOCK,
+                final=True, bounds=(part * heads_part, (part + 1) * heads_part),
+            )
+            return carry
+
+        lax.fori_loop(0, parts, one_part, 0)
+
+    @pl.when(jnp.logical_not(both_exist))
+    def _():
+        for bit, side, waited in late:
+            band(bit, side, waited)
+
+        def finish(head, carry):
+            cols = pl.ds(pl.multiple_of(head * HEAD, HEAD), HEAD)
+            o_ref[:, cols] = (mixed[head] / total[head]).astype(o_ref.dtype)
+            return carry
+
+        lax.fori_loop(0, heads, finish, 0)
 
     for side, delta in ((0, 1), (1, -1)):
 
@@ -319,16 +355,18 @@
 
             @pl.when(pred)
             def _(bit=bit, side=side, device=device):
-                for chunk in range(chunks):
-                    band_copy(bit, side, chunk, device).wait_send()
+                for part in range(parts):
+                    for copy in band_copies(bit, side, part, device):
+                        copy.wait_send()
 
     if relayed:
         for pred, make in relay_pair:
 
             @pl.when(pred)
             def _(make=make):
-                for chunk in range(chunks):
-                    make(chunk).wait_send()
+                for part in range(parts):
+                    for copy in make(part):
+                        copy.wait_send()
 
 
 def shards(tm_count, space_count, queries, key_rows, value_rows, block_list, block_count):
@@ -338,11 +376,12 @@
     heads = width // HEAD
     slots = 2 * (tm_count.bit_length() - 1)
     kind = key_rows.dtype
+    parts = math.gcd(heads, 6)
     anywhere = pl.BlockSpec(memory_space=pl.ANY)
     scalar = pl.BlockSpec(memory_space=pltpu.SMEM)
     dma = pltpu.SemaphoreType.DMA
     return pl.pallas_call(
-        functools.partial(kernel, tm_count, space_count, block_list.shape[1]),
+        functools.partial(kernel, tm_count, space_count, block_list.shape[1], parts),
         out_shape=jax.ShapeDtypeStruct((rows, width), queries.dtype),
         in_specs=[anywhere, anywhere, anywhere, scalar, scalar],
         out_specs=pl.BlockSpec(memory_space=pltpu.VMEM),
@@ -352,8 +391,8 @@
             pltpu.VMEM((rows, width), kind),
             pltpu.VMEM((2, BLOCK, width), kind),
             pltpu.VMEM((2, BLOCK, width), kind),
-            pltpu.VMEM((slots, picks * BLOCK, width), kind),
-            pltpu.VMEM((slots, picks * BLOCK, width), kind),
+            pltpu.VMEM((slots, picks, BLOCK, width), kind),
+            pltpu.VMEM((slots, picks, BLOCK, width), kind),
             pltpu.VMEM((heads, rows, HEAD), jnp.float32),
             pltpu.VMEM((heads, rows, HEAD), jnp.float32),
             pltpu.VMEM((heads, rows, HEAD), jnp.float32),
@@ -362,9 +401,9 @@
             dma((3,)),
             dma((2, 2)),
             dma((2, 2)),
-            dma((slots, 2 * picks)),
-            dma((slots, 2 * picks)),
-            dma((2, 2 * picks)),
+            dma((slots, parts, 2)),
+            dma((slots, parts, 2)),
+            dma((2, parts, 2)),
         ],
         compiler_params=pltpu.CompilerParams(
             collective_id=0, has_side_effects=True, vmem_limit_bytes=60 * 1024 * 1024

time: 88.8 us -> 79.2 us (0.89); the launches traced: 87.6 us -> 79 us
  Pallas kernels: 84.9 us -> 76.4 us
    pallas_call x1, Pallas kernels: 84.9 us -> 76.4 us  [shards(): pl.pallas_call(functools.partial(kernel, tm_count, space_count, block_lis...]
where the time goes in v2:
time: 79.2 us; the launch traced here: 79 us
  Pallas kernels  76.4 us (96%)
  local copies, waits for them, and re-layouts  2.65 us (3%)
    pallas_call x1, Pallas kernels, shards(): pl.pallas_call(functools.partial(kernel, tm_count, space_count, block_lis...  76.4 us
    unnamed x1, local copies, waits for them, and re-layouts  2.65 us

profile of v2, /device:TPU:18, one launch (start us, length us, event | category | flops | bytes accessed | tf_op | source)
XLA Modules:
  0.0 79.0 jit_solution(6329310005337687042)
XLA Ops:
  0.0 76.4 %shard_map.55 = bf16[512,1536]{1,0:T(8,128)(2,1)} custom-call(bf16[512,1536]{1,0:T(8,128)(2,1)} %q_hbm.1, bf16[512,1536]{1,0:T(8,128)(2,1)} %k_hbm.1, bf16[512,1536]{1,0:T(8,128)(2,1)} %v_hbm.1, s32[4,8]{1,0:T(4,128)} %list_ref.1, s32[4]{0:T(128)} %count_ref.1), custom_call_target="tpu_custom_call" | custom-call | tf_op jit(solution)/shard_map/pallas_call | solution.py:383
  76.4 2.7 %copy.7 = bf16[512,1536]{1,0:T(8,128)(2,1)} copy(bf16[512,1536]{1,0:T(8,128)(2,1)} %shard_map.55) | data formatting | bytes 3145728

commit v3 on v2

--- a/solution.py
+++ b/solution.py
@@ -16,7 +16,8 @@
 
 def kernel(
     tm_count, space_count, list_width, parts,
-    q_hbm, k_hbm, v_hbm, list_ref, count_ref, o_ref,
+    q_hbm, k_hbm, v_hbm, list_hbm, count_hbm, o_ref,
+    list_ref, count_ref,
     q_own, k_own, v_own, k_halo, v_halo, k_band, v_band,
     top, total, mixed, near_bias, band_bias,
     local_sem, halo_send, halo_recv, band_send, band_recv, relay_send,
@@ -41,68 +42,6 @@
     def slab_exists(delta):
         return (slab + delta >= 0) & (slab + delta < space_count)
 
-    barrier = pltpu.get_barrier_semaphore()
-    greets = []
-    for delta in (-1, 1):
-        greets.append((slab_exists(delta), {"space": slab + delta}))
-    for bit in range(bits):
-        for delta in (-(1 << bit), 1 << bit):
-            greets.append((exists(delta), {"tm": frame + delta}))
-    if relayed:
-        greets.append((frame == 0, {"tm": frame + half - 1}))
-        greets.append((frame == half - 1, {"tm": frame - half + 1}))
-        greets.append((frame == tm_count - 1, {"tm": frame - half + 1}))
-        greets.append((frame == half, {"tm": frame + half - 1}))
-    expected = 0
-    for pred, device in greets:
-        expected = expected + flag(pred)
-
-        @pl.when(pred)
-        def _(device=device):
-            pl.semaphore_signal(barrier, inc=1, device_id=device, device_id_type=MESH)
-
-    pl.semaphore_wait(barrier, expected)
-
-    def halo_copies(side, delta):
-        start = (blocks - 1) * BLOCK if side == 0 else 0
-        for index, (src, dst) in enumerate(((k_hbm, k_halo), (v_hbm, v_halo))):
-            yield pltpu.make_async_remote_copy(
-                src_ref=src.at[pl.ds(start, BLOCK)],
-                dst_ref=dst.at[side],
-                send_sem=halo_send.at[side, index],
-                recv_sem=halo_recv.at[side, index],
-                device_id={"space": slab + delta},
-                device_id_type=MESH,
-            )
-
-    part_width = width // parts
-
-    def part_cols(part):
-        return pl.ds(pl.multiple_of(part * part_width, part_width), part_width)
-
-    def band_copies(bit, side, part, device):
-        slot = 2 * bit + side
-        for which, (src, dst) in enumerate(((k_hbm, k_band), (v_hbm, v_band))):
-            yield pltpu.make_async_remote_copy(
-                src_ref=src.reshape(picks, 2, BLOCK, width).at[:, bit % 2, :, part_cols(part)],
-                dst_ref=dst.at[slot, :, :, part_cols(part)],
-                send_sem=band_send.at[slot, part, which],
-                recv_sem=band_recv.at[slot, part, which],
-                device_id={"tm": device},
-                device_id_type=MESH,
-            )
-
-    def relay_copies(kind, slot_from, slot_to, part, device):
-        for which, buf in enumerate((k_band, v_band)):
-            yield pltpu.make_async_remote_copy(
-                src_ref=buf.at[slot_from, :, :, part_cols(part)],
-                dst_ref=buf.at[slot_to, :, :, part_cols(part)],
-                send_sem=relay_send.at[kind, part, which],
-                recv_sem=band_recv.at[slot_to, part, which],
-                device_id={"tm": device},
-                device_id_type=MESH,
-            )
-
     def sends(bit, side):
         delta = (1 << bit) if side == 0 else -(1 << bit)
         pred = exists(delta)
@@ -115,6 +54,69 @@
                 pred = pred & ((frame < half) | (frame >= half + 2))
         return pred, frame + delta
 
+    barrier = pltpu.get_barrier_semaphore()
+    greets = []
+    for delta in (-1, 1):
+        greets.append((slab_exists(delta), {"space": slab + delta}))
+    for bit in range(bits):
+        for side in (0, 1):
+            pred, device = sends(bit, side)
+            greets.append((pred, {"tm": device}))
+    if relayed:
+        greets.append((frame == 0, {"tm": frame + half - 1}))
+        greets.append((frame == half - 1, {"tm": frame - half + 1}))
+        greets.append((frame == tm_count - 1, {"tm": frame - half + 1}))
+        greets.append((frame == half, {"tm": frame + half - 1}))
+    expected = 0
+    for pred, device in greets:
+        expected = expected + flag(pred)
+
+        @pl.when(pred)
+        def _(device=device):
+            pl.semaphore_signal(barrier, inc=1, device_id=device, device_id_type=MESH)
+
+    pl.semaphore_wait(barrier, expected)
+
+    def halo_copies(side, delta):
+        start = (blocks - 1) * BLOCK if side == 0 else 0
+        for index, (src, dst) in enumerate(((k_hbm, k_halo), (v_hbm, v_halo))):
+            yield pltpu.make_async_remote_copy(
+                src_ref=src.at[pl.ds(start, BLOCK)],
+                dst_ref=dst.at[side],
+                send_sem=halo_send.at[side, index],
+                recv_sem=halo_recv.at[side, index],
+                device_id={"space": slab + delta},
+                device_id_type=MESH,
+            )
+
+    part_width = width // parts
+
+    def part_cols(part):
+        return pl.ds(pl.multiple_of(part * part_width, part_width), part_width)
+
+    def band_copies(bit, side, part, device):
+        slot = 2 * bit + side
+        for which, (src, dst) in enumerate(((k_hbm, k_band), (v_hbm, v_band))):
+            yield pltpu.make_async_remote_copy(
+                src_ref=src.reshape(picks, 2, BLOCK, width).at[:, bit % 2, :, part_cols(part)],
+                dst_ref=dst.at[slot, :, :, part_cols(part)],
+                send_sem=band_send.at[slot, part, which],
+                recv_sem=band_recv.at[slot, part, which],
+                device_id={"tm": device},
+                device_id_type=MESH,
+            )
+
+    def relay_copies(kind, slot_from, slot_to, part, device):
+        for which, buf in enumerate((k_band, v_band)):
+            yield pltpu.make_async_remote_copy(
+                src_ref=buf.at[slot_from, :, :, part_cols(part)],
+                dst_ref=buf.at[slot_to, :, :, part_cols(part)],
+                send_sem=relay_send.at[kind, part, which],
+                recv_sem=band_recv.at[slot_to, part, which],
+                device_id={"tm": device},
+                device_id_type=MESH,
+            )
+
     for side, delta in ((0, 1), (1, -1)):
 
         @pl.when(slab_exists(delta))
@@ -135,10 +137,16 @@
 
     local = [
         pltpu.make_async_copy(src, dst, local_sem.at[index])
-        for index, (src, dst) in enumerate(((q_hbm, q_own), (k_hbm, k_own), (v_hbm, v_own)))
+        for index, (src, dst) in enumerate((
+            (q_hbm, q_own), (k_hbm, k_own), (v_hbm, v_own),
+            (list_hbm, list_ref), (count_hbm, count_ref),
+        ))
     ]
     for copy in local:
         copy.start()
+
+    for copy in local[3:]:
+        copy.wait()
 
     frame_blocks = blocks * space_count
     first_block = frame * frame_blocks + slab * blocks
@@ -168,7 +176,7 @@
             for tile, value in enumerate(bias_rows(ids)):
                 band_bias[2 * bit + side, tile : tile + 1, :] = value
 
-    for copy in local:
+    for copy in local[:3]:
         copy.wait()
 
     def attend(get_k, get_v, get_bias, keys, first=False, final=False, bounds=None):
@@ -377,15 +385,16 @@
     slots = 2 * (tm_count.bit_length() - 1)
     kind = key_rows.dtype
     parts = math.gcd(heads, 6)
-    anywhere = pl.BlockSpec(memory_space=pl.ANY)
-    scalar = pl.BlockSpec(memory_space=pltpu.SMEM)
+    in_hbm = pl.BlockSpec(memory_space=pltpu.HBM)
     dma = pltpu.SemaphoreType.DMA
     return pl.pallas_call(
         functools.partial(kernel, tm_count, space_count, block_list.shape[1], parts),
         out_shape=jax.ShapeDtypeStruct((rows, width), queries.dtype),
-        in_specs=[anywhere, anywhere, anywhere, scalar, scalar],
+        in_specs=[in_hbm] * 5,
         out_specs=pl.BlockSpec(memory_space=pltpu.VMEM),
         scratch_shapes=[
+            pltpu.SMEM(block_list.shape, block_list.dtype),
+            pltpu.SMEM(block_count.shape, block_count.dtype),
             pltpu.VMEM((rows, width), kind),
             pltpu.VMEM((rows, width), kind),
             pltpu.VMEM((rows, width), kind),
@@ -398,7 +407,7 @@
             pltpu.VMEM((heads, rows, HEAD), jnp.float32),
             pltpu.VMEM((blocks, (blocks + 2) * BLOCK), jnp.float32),
             pltpu.VMEM((slots, blocks, picks * BLOCK), jnp.float32),
-            dma((3,)),
+            dma((5,)),
             dma((2, 2)),
             dma((2, 2)),
             dma((slots, parts, 2)),
@@ -406,9 +415,12 @@
             dma((2, parts, 2)),
         ],
         compiler_params=pltpu.CompilerParams(
-            collective_id=0, has_side_effects=True, vmem_limit_bytes=60 * 1024 * 1024
+            collective_id=0, has_side_effects=True, vmem_limit_bytes=44 * 1024 * 1024
         ),
-    )(queries, key_rows, value_rows, block_list, block_count)
+    )(*[
+        pltpu.with_memory_space_constraint(array, pltpu.HBM)
+        for array in (queries, key_rows, value_rows, block_list, block_count)
+    ])
 
 
 def solution(mesh):

time: 79.2 us -> 75.8 us (0.957)
  Pallas kernels: 76.4 us -> 74.5 us
  local copies, waits for them, and re-layouts: 2.65 us -> 1.15 us
    pallas_call x1, Pallas kernels: 76.4 us -> 74.5 us  [shards(): pl.pallas_call(functools.partial(kernel, tm_count, space_count, block_lis...]
    unnamed x1, local copies, waits for them, and re-layouts: 2.65 us -> 1.15 us
where the time goes in v3:
time: 75.8 us; the launch traced here: 75.7 us
  Pallas kernels  74.5 us (98%)
  local copies, waits for them, and re-layouts  1.15 us (2%)
    pallas_call x1, Pallas kernels, shards(): pl.pallas_call(functools.partial(kernel, tm_count, space_count, block_lis...  74.5 us

profile of v3, /device:TPU:18, one launch (start us, length us, event | category | flops | bytes accessed | tf_op | source)
XLA Modules:
  0.0 75.7 jit_solution(11355832489329896466)
XLA Ops:
  0.0 74.5 %shard_map.55 = bf16[512,1536]{1,0:T(8,128)(2,1)S(1)} custom-call(bf16[512,1536]{1,0:T(8,128)(2,1)} %q_hbm.1, bf16[512,1536]{1,0:T(8,128)(2,1)} %k_hbm.1, bf16[512,1536]{1,0:T(8,128)(2,1)} %v_hbm.1, s32[4,8]{1,0:T(4,128)} %list_hbm.1, s32[4]{0:T(128)} %count_hbm.1), custom_call_target="tpu_custom_call" | custom-call | tf_op jit(solution)/shard_map/pallas_call | solution.py:390
  74.5 1.1 %copy.7 = bf16[512,1536]{1,0:T(8,128)(2,1)} copy(bf16[512,1536]{1,0:T(8,128)(2,1)S(1)} %shard_map.55) | data formatting | bytes 3145728

commit v4 on v3

--- a/solution.py
+++ b/solution.py
@@ -14,8 +14,17 @@
 MESH = pl.DeviceIdType.MESH
 
 
+def head_spans(heads):
+    spans, start = [], 0
+    while start < heads:
+        count = max(1, (heads - start) // 2)
+        spans.append((start, count))
+        start += count
+    return spans
+
+
 def kernel(
-    tm_count, space_count, list_width, parts,
+    tm_count, space_count, list_width,
     q_hbm, k_hbm, v_hbm, list_hbm, count_hbm, o_ref,
     list_ref, count_ref,
     q_own, k_own, v_own, k_halo, v_halo, k_band, v_band,
@@ -89,10 +98,12 @@
                 device_id_type=MESH,
             )
 
-    part_width = width // parts
+    spans = head_spans(heads)
+    parts = len(spans)
 
     def part_cols(part):
-        return pl.ds(pl.multiple_of(part * part_width, part_width), part_width)
+        start, count = spans[part]
+        return pl.ds(start * HEAD, count * HEAD)
 
     def band_copies(bit, side, part, device):
         slot = 2 * bit + side
@@ -220,8 +231,12 @@
                     total[head] = new_total
             return carry
 
-        low, high = (0, heads) if bounds is None else bounds
-        lax.fori_loop(low, high, one_head, 0)
+        start, count = (0, heads) if bounds is None else bounds
+        paired = count - count % 2
+        if paired > 2:
+            lax.fori_loop(start, start + paired, one_head, 0, unroll=2)
+        for head in range(start if paired <= 2 else start + paired, start + count):
+            one_head(head, 0)
 
     attend(
         lambda cols: k_own[:, cols],
@@ -323,20 +338,17 @@
         def joined(index, axis):
             return lambda arg: jnp.concatenate([g[index](arg) for g in getters], axis=axis)
 
-        def one_part(part, carry):
+        for part in range(parts):
             for bit, side, waited in late:
 
                 @pl.when(jnp.logical_not(waited))
-                def _(bit=bit, side=side):
+                def _(bit=bit, side=side, part=part):
                     band_wait(bit, side, part)
 
             attend(
                 joined(0, 0), joined(1, 0), joined(2, 1), 2 * picks * BLOCK,
-                final=True, bounds=(part * heads_part, (part + 1) * heads_part),
-            )
-            return carry
-
-        lax.fori_loop(0, parts, one_part, 0)
+                final=True, bounds=spans[part],
+            )
 
     @pl.when(jnp.logical_not(both_exist))
     def _():
@@ -384,11 +396,11 @@
     heads = width // HEAD
     slots = 2 * (tm_count.bit_length() - 1)
     kind = key_rows.dtype
-    parts = math.gcd(heads, 6)
+    parts = len(head_spans(heads))
     in_hbm = pl.BlockSpec(memory_space=pltpu.HBM)
     dma = pltpu.SemaphoreType.DMA
     return pl.pallas_call(
-        functools.partial(kernel, tm_count, space_count, block_list.shape[1], parts),
+        functools.partial(kernel, tm_count, space_count, block_list.shape[1]),
         out_shape=jax.ShapeDtypeStruct((rows, width), queries.dtype),
         in_specs=[in_hbm] * 5,
         out_specs=pl.BlockSpec(memory_space=pltpu.VMEM),

time: 75.8 us -> 74.7 us (0.985)
  Pallas kernels: 74.5 us -> 73.4 us
    pallas_call x1, Pallas kernels: 74.5 us -> 73.4 us  [shards(): pl.pallas_call(functools.partial(kernel, tm_count, space_count, block_lis...]
where the time goes in v4:
time: 74.7 us; the launch traced here: 74.6 us
  Pallas kernels  73.4 us (98%)
  local copies, waits for them, and re-layouts  1.15 us (2%)
    pallas_call x1, Pallas kernels, shards(): pl.pallas_call(functools.partial(kernel, tm_count, space_count, block_lis...  73.4 us

profile of v4, /device:TPU:18, one launch (start us, length us, event | category | flops | bytes accessed | tf_op | source)
XLA Modules:
  0.0 74.6 jit_solution(3511968203829120737)
XLA Ops:
  0.0 73.4 %shard_map.55 = bf16[512,1536]{1,0:T(8,128)(2,1)S(1)} custom-call(bf16[512,1536]{1,0:T(8,128)(2,1)} %q_hbm.1, bf16[512,1536]{1,0:T(8,128)(2,1)} %k_hbm.1, bf16[512,1536]{1,0:T(8,128)(2,1)} %v_hbm.1, s32[4,8]{1,0:T(4,128)} %list_hbm.1, s32[4]{0:T(128)} %count_hbm.1), custom_call_target="tpu_custom_call" | custom-call | tf_op jit(solution)/shard_map/pallas_call | solution.py:402
  73.4 1.1 %copy.7 = bf16[512,1536]{1,0:T(8,128)(2,1)} copy(bf16[512,1536]{1,0:T(8,128)(2,1)S(1)} %shard_map.55) | data formatting | bytes 3145728
